TPU v7x, 32 devices: a whole 2x2x4 slice. The times are simulated.
32 devices in a mesh: sx: 8 (over y, x, core), sy: 4 (over z).
Axes of the slice: x: 2, y: 2, z: 4, core: 2. Of those that a mesh axis runs over, the one named last changes fastest.
Arguments:
- sources: bfloat16 [8, 4, 2, 64, 4096], P('sx', 'sy'), may hold values from -6 to 6
- translate_re: bfloat16 [4, 2, 2, 64, 64], replicated, may hold values from -0.375 to 0.375
- translate_im: bfloat16 [4, 2, 2, 64, 64], replicated, may hold values from -0.375 to 0.375
- frame_index: int32 [8, 4, 16], P('sx', 'sy'), may hold values from 0 to 4095
- velocity_index: int32 [8, 4, 256], P('sx', 'sy'), may hold values from 0 to 4095
- eval_re: bfloat16 [64, 64], replicated, may hold values from -1.5 to 1.5
- eval_im: bfloat16 [64, 64], replicated, may hold values from -1.5 to 1.5
- window: int32 [8, 4], P('sx', 'sy'), may hold values from 1 to 2
Outputs:
- smoothed: bfloat16 [64, 32, 4096], P('sx', 'sy')
All inputs are finite; a program needn't handle non-finite values.
Results may differ from a plain program's by a relative error of at most 0.0076.
Values may be sent and summed in bfloat16 or wider, within the bound.
A program may use at most 64 MiB of HBM per device.

v0:
```python
import math

import jax
import jax.numpy as jnp
from jax import lax
from jax.sharding import PartitionSpec as P

LEVELS = 4
VGRID = 4096


TWO_PI = 2.0 * math.pi


def swapped(block, axis, bit):
    count = lax.axis_size(axis)
    route = []
    for low in range(count):
        high = low | 1 << bit
        if high != low and high < count:
            route += [(low, high), (high, low)]
    return lax.ppermute(block, axis, route)


def with_halo(block, sides, width):
    for axis, dim in sides:
        count = lax.axis_size(axis)
        forward = [(i, i + 1) for i in range(count - 1)]
        backward = [(target, source) for source, target in forward]
        low = lax.ppermute(
            lax.slice_in_dim(block, block.shape[dim] - width, None, axis=dim), axis, forward
        )
        high = lax.ppermute(lax.slice_in_dim(block, 0, width, axis=dim), axis, backward)
        block = jnp.concatenate([low, block, high], axis=dim)
    return block


def blocks(real_part, imag_part):
    upper = jnp.concatenate([real_part, -imag_part], axis=-1)
    lower = jnp.concatenate([imag_part, real_part], axis=-1)
    return jnp.concatenate([upper, lower], axis=-2)


def on_device(
    sources, translate_re, translate_im, frame_index, velocity_index, eval_re, eval_im, window
):
    terms = sources.shape[3]
    columns = sources.shape[4]
    state_flat = sources[0, 0].reshape(2 * terms, columns)
    base_product = frame_index[0, 0][:, None] * velocity_index[0, 0][None, :]
    for level_no in range(LEVELS):
        if level_no % 2 == 0:
            bit_pos = lax.axis_size("sx").bit_length() - 2 - level_no // 2
            own_bit = lax.axis_index("sx") >> bit_pos & 1
        else:
            bit_pos = lax.axis_size("sy").bit_length() - 2 - level_no // 2
            own_bit = lax.axis_index("sy") >> bit_pos & 1
        self_matrix = blocks(translate_re[level_no, own_bit, 0], translate_im[level_no, own_bit, 0])
        own_part = jnp.dot(self_matrix, state_flat, preferred_element_type=jnp.float32)
        if level_no % 2 == 0:
            received = swapped(state_flat, "sx", bit_pos)
        else:
            received = swapped(state_flat, "sy", bit_pos)
        other_matrix = blocks(
            translate_re[level_no, own_bit, 1], translate_im[level_no, own_bit, 1]
        )
        total = own_part + jnp.dot(other_matrix, received, preferred_element_type=jnp.float32)
        product = base_product * (level_no + 1) % VGRID
        angles = (TWO_PI / VGRID * product.astype(jnp.float32)).reshape(columns)
        cosine = jnp.cos(angles)[None, :]
        sine_part = jnp.sin(angles)[None, :]
        real_total = total[:terms]
        imag_total = total[terms:]
        new_real = cosine * real_total - sine_part * imag_total
        new_imag = sine_part * real_total + cosine * imag_total
        state_flat = jnp.concatenate([new_real, new_imag], axis=0).astype(jnp.bfloat16)
    evaluate = jnp.concatenate([eval_re, -eval_im], axis=1)
    side = math.isqrt(eval_re.shape[0])
    picture = jnp.dot(evaluate, state_flat, preferred_element_type=jnp.float32).astype(jnp.bfloat16)
    picture = picture.reshape(side, side, columns)
    padded = with_halo(picture, (("sx", 0), ("sy", 1)), 2)
    values = padded.astype(jnp.float32)
    rows_near = values[1:-3] + values[2:-2] + values[3:-1]
    rows_far = rows_near + values[0:-4] + values[4:]
    box_near = rows_near[:, 1:-3] + rows_near[:, 2:-2] + rows_near[:, 3:-1]
    box_far = (
        rows_far[:, 1:-3]
        + rows_far[:, 2:-2]
        + rows_far[:, 3:-1]
        + rows_far[:, 0:-4]
        + rows_far[:, 4:]
    )
    chosen = jnp.where(window[0, 0] == 2, box_far / 25.0, box_near / 9.0)
    return chosen.astype(jnp.bfloat16)


def solution(mesh):
    return jax.shard_map(
        on_device,
        mesh=mesh,
        in_specs=(
            P("sx", "sy", None, None, None),
            P(),
            P(),
            P("sx", "sy", None),
            P("sx", "sy", None),
            P(),
            P(),
            P("sx", "sy"),
        ),
        out_specs=P("sx", "sy", None),
        check_vma=False,
    )
```

profile of v0, /device:TPU:20, one launch (start us, length us, event | category | flops | bytes accessed | tf_op | source)
XLA Modules:
  0.0 152.3 jit_solution(4088940862716622229)
XLA Ops:
  0.0 0.5 collective-permute-start
  0.5 0.8 multiply_bitcast_fusion
  1.3 0.9 dynamic-slice_bitcast_fusion.1
  2.1 0.9 fusion.99
  3.0 0.3 fusion.89
  3.3 1.7 %fusion.31 = f32[128,4096]{1,0:T(8,128)S(1)} fusion(bf16[128,4096]{1,0:T(8,128)(2,1)} %bitcast.59, bf16[64,64]{1,0:T(8,128)(2,1)S(1)} %get-tuple-element.52, bf16[64,64]{1,0:T(8,128)(2,1)S(1)} %get-tuple-element.40, bf16[64,64]{1,0:T(8,128)(2,1)S(1)} %get-tuple-element.39), kind=kOutput, calls=%fused_computation.63 | convolution fusion | flops 134348800 | bytes 3170304 | tf_op jit(solution)/shard_map/dot_general | solution.py:59
  5.0 20.1 %collective-permute-done = bf16[128,4096]{1,0:T(8,128)(2,1)S(1)} collective-permute-done((bf16[128,4096]{1,0:T(8,128)(2,1)}, bf16[128,4096]{1,0:T(8,128)(2,1)S(1)}, u32[]{:S(2)}, u32[]{:S(2)}) %collective-permute-start) | collective-permute-done | bytes 1048608 | tf_op jit(solution)/shard_map/ppermute | solution.py:22
  25.1 0.5 convolution_add_fusion.3
  25.6 0.3 subtract_convert_fusion.3
  25.9 0.1 pad_maximum_fusion
  26.0 0.4 collective-permute-start.1
  26.4 0.5 fusion.23
  26.9 43.5 %collective-permute-done.1 = bf16[128,4096]{1,0:T(8,128)(2,1)S(1)} collective-permute-done((bf16[128,4096]{1,0:T(8,128)(2,1)S(1)}, bf16[128,4096]{1,0:T(8,128)(2,1)S(1)}, u32[]{:S(2)}, u32[]{:S(2)}) %collective-permute-start.1) | collective-permute-done | bytes 1048608 | tf_op jit(solution)/shard_map/ppermute | solution.py:22
  70.4 0.5 convolution_add_fusion.2
  70.9 0.3 subtract_convert_fusion.2
  71.1 0.1 pad_maximum_fusion.1
  71.2 1.6 %collective-permute-start.2 = (bf16[128,4096]{1,0:T(8,128)(2,1)S(1)}, bf16[128,4096]{1,0:T(8,128)(2,1)S(1)}, u32[]{:S(2)}, u32[]{:S(2)}) collective-permute-start(bf16[128,4096]{1,0:T(8,128)(2,1)S(1)} %pad_maximum_fusion.1), channel_id=1, source_target_pairs={{0,8},{8,0},{4,12},{12,4},{16,24},{24,16},{20,28},{28,20},{1,9},{9... | collective-permute-start | bytes 3145736 | tf_op jit(solution)/shard_map/ppermute | solution.py:22
  72.8 0.5 fusion.15
  73.3 22.1 %collective-permute-done.2 = bf16[128,4096]{1,0:T(8,128)(2,1)S(1)} collective-permute-done((bf16[128,4096]{1,0:T(8,128)(2,1)S(1)}, bf16[128,4096]{1,0:T(8,128)(2,1)S(1)}, u32[]{:S(2)}, u32[]{:S(2)}) %collective-permute-start.2) | collective-permute-done | bytes 1048608 | tf_op jit(solution)/shard_map/ppermute | solution.py:22
  95.4 0.5 convolution_add_fusion.1
  95.9 0.0 copy-start
  95.9 0.3 subtract_convert_fusion.1
  96.1 0.1 pad_maximum_fusion.2
  96.2 5.6 %collective-permute-start.3 = (bf16[128,4096]{1,0:T(8,128)(2,1)S(1)}, bf16[128,4096]{1,0:T(8,128)(2,1)S(1)}, u32[]{:S(2)}, u32[]{:S(2)}) collective-permute-start(bf16[128,4096]{1,0:T(8,128)(2,1)S(1)} %pad_maximum_fusion.2), channel_id=1, source_target_pairs={{0,1},{1,0},{2,3},{3,2},{4,5},{5,4},{6,7},{7,6},{8,9},{9,8},{10,11... | collective-permute-start | bytes 3145736 | tf_op jit(solution)/shard_map/ppermute | solution.py:22
  101.8 0.0 copy-done
  101.9 0.5 fusion.7
  102.3 22.0 %collective-permute-done.3 = bf16[128,4096]{1,0:T(8,128)(2,1)S(1)} collective-permute-done((bf16[128,4096]{1,0:T(8,128)(2,1)S(1)}, bf16[128,4096]{1,0:T(8,128)(2,1)S(1)}, u32[]{:S(2)}, u32[]{:S(2)}) %collective-permute-start.3) | collective-permute-done | bytes 1048608 | tf_op jit(solution)/shard_map/ppermute | solution.py:22
  124.3 0.5 convolution_add_fusion
  124.8 0.0 copy-start.1
  124.8 0.3 subtract_convert_fusion
  125.1 0.4 copy-done.1
  125.5 0.4 convolution_convert_fusion
  125.9 0.1 copy.9
  126.1 1.9 %collective-permute-start.4 = (bf16[2,8,4096]{2,0,1:T(2,128)(2,1)S(1)}, bf16[2,8,4096]{2,0,1:T(2,128)(2,1)S(1)}, u32[]{:S(2)}, u32[]{:S(2)}) collective-permute-start(bf16[2,8,4096]{2,0,1:T(2,128)(2,1)S(1)} %copy.9), channel_id=1, source_target_pairs={{0,4},{4,8},{8,12},{12,16},{16,20},{20,24},{24,28},{1,5},{5,9},{9,... | collective-permute-start | bytes 393224 | tf_op jit(solution)/shard_map/ppermute | solution.py:30
  128.0 0.1 copy.10
  128.1 4.5 %collective-permute-start.5 = (bf16[2,8,4096]{2,0,1:T(2,128)(2,1)S(1)}, bf16[2,8,4096]{2,0,1:T(2,128)(2,1)S(1)}, u32[]{:S(2)}, u32[]{:S(2)}) collective-permute-start(bf16[2,8,4096]{2,0,1:T(2,128)(2,1)S(1)} %copy.10), channel_id=1, source_target_pairs={{4,0},{8,4},{12,8},{16,12},{20,16},{24,20},{28,24},{5,1},{9,5},{13... | collective-permute-start | bytes 393224 | tf_op jit(solution)/shard_map/ppermute | solution.py:33
  132.7 0.3 copy.11
  133.0 0.3 collective-permute-done.4
  133.2 1.9 %collective-permute-done.5 = bf16[2,8,4096]{2,0,1:T(2,128)(2,1)S(1)} collective-permute-done((bf16[2,8,4096]{2,0,1:T(2,128)(2,1)S(1)}, bf16[2,8,4096]{2,0,1:T(2,128)(2,1)S(1)}, u32[]{:S(2)}, u32[]{:S(2)}) %collective-permute-start.5) | collective-permute-done | bytes 131104 | tf_op jit(solution)/shard_map/ppermute | solution.py:33
  135.2 0.2 pad_maximum_fusion.5
  135.4 3.7 %collective-permute-start.6 = (bf16[12,2,4096]{2,0,1:T(8,128)(2,1)S(1)}, bf16[12,2,4096]{2,0,1:T(8,128)(2,1)S(1)}, u32[]{:S(2)}, u32[]{:S(2)}) collective-permute-start(bf16[12,2,4096]{2,0,1:T(8,128)(2,1)S(1)} %get-tuple-element.31), channel_id=1, source_target_pairs={{0,1},{1,2},{2,3},{4,5},{5,6},{6,7},{8,9},{9,10},{10,11},{12,13},{... | collective-permute-start | bytes 589832 | tf_op jit(solution)/shard_map/ppermute | solution.py:30
  139.1 2.2 %collective-permute-start.7 = (bf16[12,2,4096]{2,0,1:T(8,128)(2,1)S(1)}, bf16[12,2,4096]{2,0,1:T(8,128)(2,1)S(1)}, u32[]{:S(2)}, u32[]{:S(2)}) collective-permute-start(bf16[12,2,4096]{2,0,1:T(8,128)(2,1)S(1)} %get-tuple-element.32), channel_id=1, source_target_pairs={{1,0},{2,1},{3,2},{5,4},{6,5},{7,6},{9,8},{10,9},{11,10},{13,12},{... | collective-permute-start | bytes 589832 | tf_op jit(solution)/shard_map/ppermute | solution.py:33
  141.9 4.4 %collective-permute-done.6 = bf16[12,2,4096]{2,0,1:T(8,128)(2,1)S(1)} collective-permute-done((bf16[12,2,4096]{2,0,1:T(8,128)(2,1)S(1)}, bf16[12,2,4096]{2,0,1:T(8,128)(2,1)S(1)}, u32[]{:S(2)}, u32[]{:S(2)}) %collective-permute-start.6) | collective-permute-done | bytes 196640 | tf_op jit(solution)/shard_map/ppermute | solution.py:30
  146.4 3.4 %collective-permute-done.7 = bf16[12,2,4096]{2,0,1:T(8,128)(2,1)S(1)} collective-permute-done((bf16[12,2,4096]{2,0,1:T(8,128)(2,1)S(1)}, bf16[12,2,4096]{2,0,1:T(8,128)(2,1)S(1)}, u32[]{:S(2)}, u32[]{:S(2)}) %collective-permute-start.7) | collective-permute-done | bytes 196640 | tf_op jit(solution)/shard_map/ppermute | solution.py:33
  149.7 0.5 maximum_convert_fusion
  150.3 0.6 slice_add_fusion
  150.9 0.3 fusion.2
  151.2 1.1 copy.12
  (3 shorter events, 0.0 us)
Async XLA Ops:
  0.0 25.1 %collective-permute-start = (bf16[128,4096]{1,0:T(8,128)(2,1)}, bf16[128,4096]{1,0:T(8,128)(2,1)S(1)}, u32[]{:S(2)}, u32[]{:S(2)}) collective-permute-start(bf16[128,4096]{1,0:T(8,128)(2,1)} %bitcast.58), channel_id=1, source_target_pairs={{0,16},{16,0},{4,20},{20,4},{8,24},{24,8},{12,28},{28,12},{1,17},{... | collective-permute-start | bytes 3145736 | tf_op jit(solution)/shard_map/ppermute | solution.py:22
  26.0 44.4 %collective-permute-start.1 = (bf16[128,4096]{1,0:T(8,128)(2,1)S(1)}, bf16[128,4096]{1,0:T(8,128)(2,1)S(1)}, u32[]{:S(2)}, u32[]{:S(2)}) collective-permute-start(bf16[128,4096]{1,0:T(8,128)(2,1)S(1)} %pad_maximum_fusion), channel_id=1, source_target_pairs={{0,2},{2,0},{1,3},{3,1},{4,6},{6,4},{5,7},{7,5},{8,10},{10,8},{9,1... | collective-permute-start | bytes 3145736 | tf_op jit(solution)/shard_map/ppermute | solution.py:22
  71.2 24.1 %collective-permute-start.2 = (bf16[128,4096]{1,0:T(8,128)(2,1)S(1)}, bf16[128,4096]{1,0:T(8,128)(2,1)S(1)}, u32[]{:S(2)}, u32[]{:S(2)}) collective-permute-start(bf16[128,4096]{1,0:T(8,128)(2,1)S(1)} %pad_maximum_fusion.1), channel_id=1, source_target_pairs={{0,8},{8,0},{4,12},{12,4},{16,24},{24,16},{20,28},{28,20},{1,9},{9... | collective-permute-start | bytes 3145736 | tf_op jit(solution)/shard_map/ppermute | solution.py:22
  95.9 6.0 %copy-start = (bf16[64,64]{1,0:T(8,128)(2,1)S(1)}, bf16[64,64]{1,0:T(8,128)(2,1)}, u32[]{:S(2)}) copy-start(bf16[64,64]{1,0:T(8,128)(2,1)} %param.14) | copy-start | bytes 24580
  96.2 28.1 %collective-permute-start.3 = (bf16[128,4096]{1,0:T(8,128)(2,1)S(1)}, bf16[128,4096]{1,0:T(8,128)(2,1)S(1)}, u32[]{:S(2)}, u32[]{:S(2)}) collective-permute-start(bf16[128,4096]{1,0:T(8,128)(2,1)S(1)} %pad_maximum_fusion.2), channel_id=1, source_target_pairs={{0,1},{1,0},{2,3},{3,2},{4,5},{5,4},{6,7},{7,6},{8,9},{9,8},{10,11... | collective-permute-start | bytes 3145736 | tf_op jit(solution)/shard_map/ppermute | solution.py:22
  124.8 0.7 copy-start.1
  126.1 7.2 %collective-permute-start.4 = (bf16[2,8,4096]{2,0,1:T(2,128)(2,1)S(1)}, bf16[2,8,4096]{2,0,1:T(2,128)(2,1)S(1)}, u32[]{:S(2)}, u32[]{:S(2)}) collective-permute-start(bf16[2,8,4096]{2,0,1:T(2,128)(2,1)S(1)} %copy.9), channel_id=1, source_target_pairs={{0,4},{4,8},{8,12},{12,16},{16,20},{20,24},{24,28},{1,5},{5,9},{9,... | collective-permute-start | bytes 393224 | tf_op jit(solution)/shard_map/ppermute | solution.py:30
  128.1 7.0 %collective-permute-start.5 = (bf16[2,8,4096]{2,0,1:T(2,128)(2,1)S(1)}, bf16[2,8,4096]{2,0,1:T(2,128)(2,1)S(1)}, u32[]{:S(2)}, u32[]{:S(2)}) collective-permute-start(bf16[2,8,4096]{2,0,1:T(2,128)(2,1)S(1)} %copy.10), channel_id=1, source_target_pairs={{4,0},{8,4},{12,8},{16,12},{20,16},{24,20},{28,24},{5,1},{9,5},{13... | collective-permute-start | bytes 393224 | tf_op jit(solution)/shard_map/ppermute | solution.py:33
  135.4 10.9 %collective-permute-start.6 = (bf16[12,2,4096]{2,0,1:T(8,128)(2,1)S(1)}, bf16[12,2,4096]{2,0,1:T(8,128)(2,1)S(1)}, u32[]{:S(2)}, u32[]{:S(2)}) collective-permute-start(bf16[12,2,4096]{2,0,1:T(8,128)(2,1)S(1)} %get-tuple-element.31), channel_id=1, source_target_pairs={{0,1},{1,2},{2,3},{4,5},{5,6},{6,7},{8,9},{9,10},{10,11},{12,13},{... | collective-permute-start | bytes 589832 | tf_op jit(solution)/shard_map/ppermute | solution.py:30
  139.1 10.6 %collective-permute-start.7 = (bf16[12,2,4096]{2,0,1:T(8,128)(2,1)S(1)}, bf16[12,2,4096]{2,0,1:T(8,128)(2,1)S(1)}, u32[]{:S(2)}, u32[]{:S(2)}) collective-permute-start(bf16[12,2,4096]{2,0,1:T(8,128)(2,1)S(1)} %get-tuple-element.32), channel_id=1, source_target_pairs={{1,0},{2,1},{3,2},{5,4},{6,5},{7,6},{9,8},{10,9},{11,10},{13,12},{... | collective-permute-start | bytes 589832 | tf_op jit(solution)/shard_map/ppermute | solution.py:33
where the time goes:
time: 153 us; the launch traced here: 152 us
  waiting for transfers between devices  118 us (77%)
  starting transfers between devices  20.4 us (13%)
  matrix products  5.41 us (4%)
  other arithmetic  4.93 us (3%)
  local copies, waits for them, and re-layouts  2.99 us (2%)
    ppermute x4, waiting for transfers between devices, swapped(): return lax.ppermute(block, axis, route)  108 us
    ppermute x4, starting transfers between devices, swapped(): return lax.ppermute(block, axis, route)  8.07 us
    ppermute x2, starting transfers between devices, with_halo(): lax.ppermute(lax.slice_in_dim(block, 0, width, axis=dim), axis, backward)  6.73 us
    ppermute x2, starting transfers between devices, with_halo(): lax.ppermute(lax.slice_in_dim(block, block.shape[dim] - width, None, axis...  5.57 us
    ppermute x2, waiting for transfers between devices, with_halo(): lax.ppermute(lax.slice_in_dim(block, 0, width, axis=dim), axis, backward)  5.3 us
    ppermute x2, waiting for transfers between devices, with_halo(): lax.ppermute(lax.slice_in_dim(block, block.shape[dim] - width, None, axis...  4.7 us
    dot_general x4, matrix products, on_device(): jnp.dot(self_matrix, state_flat, preferred_element_type=jnp.float32)  3.15 us
  transfers between devices with their start and end apart: 8, of which 8 were waited for; matrix products, arithmetic and copies ran while one was open for 4% of the time, Pallas kernels for 0%

commit v1 on v0

--- a/solution.py
+++ b/solution.py
@@ -1,8 +1,11 @@
+import functools
 import math
 
 import jax
 import jax.numpy as jnp
 from jax import lax
+from jax.experimental import pallas as pl
+from jax.experimental.pallas import tpu as pltpu
 from jax.sharding import PartitionSpec as P
 
 LEVELS = 4
@@ -94,9 +97,270 @@
     return chosen.astype(jnp.bfloat16)
 
 
+MESH = pl.DeviceIdType.MESH
+LANES = 128
+
+
+def flipped(index, mask, total):
+    bit = 1
+    while bit < total:
+        if mask & bit:
+            index = index + bit - 2 * bit * (index // bit % 2)
+        bit *= 2
+    return index
+
+
+def spread_kernel(
+    nx,
+    ny,
+    src,
+    extra,
+    re_ref,
+    im_ref,
+    ere_ref,
+    eim_ref,
+    out,
+    state,
+    extras,
+    mats,
+    picture,
+    tiles,
+    rotors,
+    send_sem,
+    recv_sem,
+    extra_send,
+    extra_recv,
+    out_send,
+    out_recv,
+):
+    total_devices = nx * ny
+    me = lax.axis_index("sx") * ny + lax.axis_index("sy")
+    rows = src.shape[0]
+    terms = rows // 2
+    side = out.shape[0]
+    columns = pl.ds(pl.multiple_of(me * LANES, LANES), LANES)
+
+    barrier = pltpu.get_barrier_semaphore()
+
+    @pl.loop(1, total_devices)
+    def _(step):
+        peer = lax.rem(me + step, total_devices)
+        pl.semaphore_signal(
+            barrier, inc=1, device_id=(peer // ny, lax.rem(peer, ny)), device_id_type=MESH
+        )
+
+    pl.semaphore_wait(barrier, total_devices - 1)
+
+    half = ny // 2
+    order = sorted(range(1, total_devices), key=lambda mask: (0 if mask & half else 1, mask))
+    sends = []
+    for mask in order:
+        peer = flipped(me, mask, total_devices)
+        where = (peer // ny, lax.rem(peer, ny))
+        theirs = pl.ds(pl.multiple_of(peer * LANES, LANES), LANES)
+        small = pltpu.make_async_remote_copy(
+            src_ref=extra.at[peer],
+            dst_ref=extras.at[me],
+            send_sem=extra_send.at[mask],
+            recv_sem=extra_recv.at[me],
+            device_id=where,
+            device_id_type=MESH,
+        )
+        large = pltpu.make_async_remote_copy(
+            src_ref=src.at[:, theirs],
+            dst_ref=state.at[me],
+            send_sem=send_sem.at[mask],
+            recv_sem=recv_sem.at[me],
+            device_id=where,
+            device_id_type=MESH,
+        )
+        small.start()
+        large.start()
+        sends += [small, large]
+    pltpu.make_async_copy(extra.at[me], extras.at[me], extra_recv.at[me]).start()
+    pltpu.make_async_copy(src.at[:, columns], state.at[me], recv_sem.at[me]).start()
+
+    for level in range(LEVELS):
+        for bit in range(2):
+            for term in range(2):
+                place = bit if term == 0 else 1 - bit
+                top = bit * rows
+                left = place * rows
+                real = re_ref[level, bit, term]
+                imag = im_ref[level, bit, term]
+                mats[level, top : top + terms, left : left + terms] = real
+                mats[level, top : top + terms, left + terms : left + rows] = -imag
+                mats[level, top + terms : top + rows, left : left + terms] = imag
+                mats[level, top + terms : top + rows, left + terms : left + rows] = real
+    evaluate = jnp.concatenate([ere_ref[...], -eim_ref[...]], axis=1)
+    picture[...] = jnp.zeros_like(picture)
+
+    @pl.loop(0, total_devices)
+    def _(box):
+        pltpu.make_async_copy(extras.at[box], extras.at[box], extra_recv.at[box]).wait()
+        cosine = extras[box, :, 0:LANES]
+        sine = extras[box, :, LANES : 2 * LANES]
+        real, imag = cosine, sine
+        for level in range(LEVELS):
+            rotors[level, 0, box] = real
+            rotors[level, 1, box] = imag
+            if level + 1 < LEVELS:
+                real, imag = real * cosine - imag * sine, real * sine + imag * cosine
+
+    def first_of(pair, stride):
+        return pair // stride * (2 * stride) + lax.rem(pair, stride)
+
+    for level in range(LEVELS):
+        axis_size = nx if level % 2 == 0 else ny
+        stride = (ny if level % 2 == 0 else 1) << (axis_size.bit_length() - 2 - level // 2)
+
+        def advance(group, _, level=level, stride=stride):
+            boxes = []
+            for part in range(2):
+                low = first_of(2 * group + part, stride)
+                boxes.append((low, low + stride))
+            if level == 0:
+                for pair in boxes:
+                    for box in pair:
+                        pltpu.make_async_copy(state.at[box], state.at[box], recv_sem.at[box]).wait()
+            stacked = jnp.concatenate(
+                [jnp.concatenate([state[low], state[high]], axis=0) for low, high in boxes], axis=1
+            )
+            sums = jnp.dot(mats[level], stacked, preferred_element_type=jnp.float32)
+            for part, pair in enumerate(boxes):
+                for bit, box in enumerate(pair):
+                    piece = sums[bit * rows : (bit + 1) * rows, part * LANES : (part + 1) * LANES]
+                    real, imag = piece[:terms], piece[terms:]
+                    cosine = rotors[level, 0, box]
+                    sine = rotors[level, 1, box]
+                    state[box, 0:terms] = (cosine * real - sine * imag).astype(jnp.bfloat16)
+                    state[box, terms:rows] = (sine * real + cosine * imag).astype(jnp.bfloat16)
+            return 0
+
+        lax.fori_loop(0, total_devices // 4, advance, 0)
+
+    def render(group, _):
+        boxes = [2 * group, 2 * group + 1]
+        stacked = jnp.concatenate([state[box] for box in boxes], axis=1)
+        cells = jnp.dot(evaluate, stacked, preferred_element_type=jnp.float32)
+        cells = cells.astype(jnp.bfloat16).astype(jnp.float32)
+        for part, box in enumerate(boxes):
+            block = cells[:, part * LANES : (part + 1) * LANES].reshape(side, side, LANES)
+            picture[pl.ds(box // ny * side + 2, side), lax.rem(box, ny) + 1] = block
+        return 0
+
+    lax.fori_loop(0, total_devices // 2, render, 0)
+
+    def smooth(box):
+        row, col = box // ny, lax.rem(box, ny)
+        values = picture[pl.ds(row * side, side + 4), pl.ds(col, 3)]
+        rows_near = values[1:-3] + values[2:-2] + values[3:-1]
+        rows_far = rows_near + values[0:-4] + values[4:]
+        rows_near = rows_near.reshape(side, 3 * side, LANES)
+        rows_far = rows_far.reshape(side, 3 * side, LANES)
+
+        def moved(block, shift):
+            return block[:, side + shift : 2 * side + shift]
+
+        box_near = moved(rows_near, -1) + moved(rows_near, 0) + moved(rows_near, 1)
+        box_far = (
+            moved(rows_far, -1)
+            + moved(rows_far, 0)
+            + moved(rows_far, 1)
+            + moved(rows_far, -2)
+            + moved(rows_far, 2)
+        )
+        wide = extras[box, :, 2 * LANES : 3 * LANES].reshape(1, 1, LANES) == 2.0
+        tiles[box] = jnp.where(wide, box_far / 25.0, box_near / 9.0).astype(jnp.bfloat16)
+
+    for mask in order:
+        peer = flipped(me, mask, total_devices)
+        smooth(peer)
+        done = pltpu.make_async_remote_copy(
+            src_ref=tiles.at[peer],
+            dst_ref=out.at[:, :, columns],
+            send_sem=out_send.at[mask],
+            recv_sem=out_recv.at[me],
+            device_id=(peer // ny, lax.rem(peer, ny)),
+            device_id_type=MESH,
+        )
+        done.start()
+        sends.append(done)
+    smooth(me)
+    pltpu.make_async_copy(tiles.at[me], out.at[:, :, columns], out_recv.at[me]).start()
+
+    for copy in sends:
+        copy.wait_send()
+
+    @pl.loop(0, total_devices)
+    def _(box):
+        pltpu.make_async_copy(tiles.at[box], tiles.at[box], out_recv.at[box]).wait()
+
+
+def spread_on_device(
+    nx,
+    ny,
+    sources,
+    translate_re,
+    translate_im,
+    frame_index,
+    velocity_index,
+    eval_re,
+    eval_im,
+    window,
+):
+    total_devices = nx * ny
+    terms, columns = sources.shape[3:]
+    rows = 2 * terms
+    side = math.isqrt(eval_re.shape[0])
+    product = frame_index[0, 0][:, None] * velocity_index[0, 0][None, :] % VGRID
+    angles = (TWO_PI / VGRID * product.astype(jnp.float32)).reshape(total_devices, 1, LANES)
+    widths = jnp.broadcast_to(window[0, 0].astype(jnp.float32), angles.shape)
+    extra = jnp.concatenate([jnp.cos(angles), jnp.sin(angles), widths], axis=-1)
+    anywhere = pl.BlockSpec(memory_space=pl.ANY)
+    inside = pl.BlockSpec(memory_space=pltpu.VMEM)
+    dma = pltpu.SemaphoreType.DMA((total_devices,))
+    return pl.pallas_call(
+        functools.partial(spread_kernel, nx, ny),
+        out_shape=jax.ShapeDtypeStruct((side, side, columns), jnp.bfloat16),
+        in_specs=[anywhere, anywhere, inside, inside, inside, inside],
+        out_specs=anywhere,
+        scratch_shapes=[
+            pltpu.VMEM((total_devices, rows, LANES), jnp.bfloat16),
+            pltpu.VMEM((total_devices, 1, 3 * LANES), jnp.float32),
+            pltpu.VMEM((LEVELS, 2 * rows, 2 * rows), jnp.bfloat16),
+            pltpu.VMEM((nx * side + 4, ny + 2, side, LANES), jnp.float32),
+            pltpu.VMEM((total_devices, side, side, LANES), jnp.bfloat16),
+            pltpu.VMEM((LEVELS, 2, total_devices, 1, LANES), jnp.float32),
+            dma,
+            dma,
+            dma,
+            dma,
+            dma,
+            dma,
+        ],
+        compiler_params=pltpu.CompilerParams(collective_id=0, has_side_effects=True),
+    )(
+        sources[0, 0].reshape(rows, columns),
+        extra,
+        translate_re,
+        translate_im,
+        eval_re,
+        eval_im,
+    )
+
+
 def solution(mesh):
+    nx, ny = mesh.shape["sx"], mesh.shape["sy"]
+
+    def body(sources, *others):
+        share, left = divmod(sources.shape[4], nx * ny)
+        if share == LANES and left == 0:
+            return spread_on_device(nx, ny, sources, *others)
+        return on_device(sources, *others)
+
     return jax.shard_map(
-        on_device,
+        body,
         mesh=mesh,
         in_specs=(
             P("sx", "sy", None, None, None),

time: 153 us -> 64.4 us (0.42)
  the two profiles are of different devices: /device:TPU:20 before, /device:TPU:0 now
where the time goes in v1:
time: 64.4 us; the launch traced here: 64.1 us
  Pallas kernels  59 us (92%)
  local copies, waits for them, and re-layouts  3.27 us (5%)
  other arithmetic  1.21 us (2%)
  between operations  0.7 us (1%)
    pallas_call x1, Pallas kernels, spread_on_device(): pl.pallas_call(functools.partial(spread_kernel, nx, ny), out_shape=jax.Sh...  59 us
    unnamed x5, local copies, waits for them, and re-layouts  3.1 us

profile of v1, /device:TPU:0, one launch (start us, length us, event | category | flops | bytes accessed | tf_op | source)
XLA Modules:
  0.0 64.1 jit_solution(2022992051254667576)
XLA Ops:
  0.7 0.0 copy-start.1
  0.7 0.6 copy-done.1
  1.3 0.1 mul.56
  1.4 0.0 copy-start
  1.4 0.1 mul.57
  1.5 0.6 copy-done
  2.1 0.1 fusion.1
  2.2 0.5 multiply_cosine_fusion
  2.6 0.7 %maximum_maximum_fusion.extra = f32[32,1,384]{2,1,0:T(1,128)} fusion(f32[32,1,128]{2,1,0:T(1,128)S(1)} %get-tuple-element.6, f32[32,1,128]{2,1,0:T(1,128)S(1)} %get-tuple-element.5, f32[384]{0:T(512)S(1)} %pad.2.clone), kind=kLoop, calls=%fused_computation | loop fusion | flops 24576 | bytes 83456 | tf_op jit(solution)/shard_map/concatenate | solution.py:319
  3.3 59.0 %shard_map.82 = bf16[8,8,4096]{2,1,0:T(8,128)(2,1)} custom-call(bf16[128,4096]{1,0:T(8,128)(2,1)} %bitcast.6, f32[32,1,384]{2,1,0:T(1,128)} %maximum_maximum_fusion.extra, bf16[4,2,2,64,64]{4,3,2,1,0:T(8,128)(2,1)} %re_ref.1, bf16[4,2,2,64,64]{4,3,2,1,0:T(8,128)(2,1)} %im_ref.1, bf16[64,64]{1,0:T(8,128)(2,1)} %ere_ref.1, bf16[64,64]{1,0:T(8,128)(2,1)} %eim_ref.1), custom_call_target="tpu_custom_call" | custom-call | tf_op jit(solution)/shard_map/pallas_call | solution.py:323
  62.3 1.9 %copy.12 = bf16[8,8,4096]{2,1,0:T(8,128)(2,1)} copy(bf16[8,8,4096]{2,1,0:T(8,128)(2,1)} %shard_map.82) | data formatting | bytes 1048576
  (3 shorter events, 0.0 us)
Async XLA Ops:
  0.7 0.7 %copy-start.1 = (s32[1,1,16]{2,1,0:T(1,128)S(1)}, s32[1,1,16]{2,1,0:T(1,128)}, u32[]{:S(2)}) copy-start(s32[1,1,16]{2,1,0:T(1,128)} %param.11) | copy-start | bytes 196
  1.4 0.7 %copy-start = (s32[1,1,256]{2,1,0:T(1,128)S(1)}, s32[1,1,256]{2,1,0:T(1,128)}, u32[]{:S(2)}) copy-start(s32[1,1,256]{2,1,0:T(1,128)} %param.12) | copy-start | bytes 3076

commit v2 on v0

--- a/solution.py
+++ b/solution.py
@@ -1,8 +1,11 @@
+import functools
 import math
 
 import jax
 import jax.numpy as jnp
 from jax import lax
+from jax.experimental import pallas as pl
+from jax.experimental.pallas import tpu as pltpu
 from jax.sharding import PartitionSpec as P
 
 LEVELS = 4
@@ -94,9 +97,375 @@
     return chosen.astype(jnp.bfloat16)
 
 
+MESH = pl.DeviceIdType.MESH
+LANES = 128
+UNROLL = 8
+
+
+def flipped(index, mask, total):
+    bit = 1
+    while bit < total:
+        if mask & bit:
+            index = index + bit - 2 * bit * (index // bit % 2)
+        bit *= 2
+    return index
+
+
+def spread_kernel(
+    nx,
+    ny,
+    src,
+    extra,
+    re_hbm,
+    im_hbm,
+    ere_hbm,
+    eim_hbm,
+    out,
+    state,
+    partial,
+    extras,
+    mats,
+    split_mats,
+    picture,
+    tiles,
+    rotors,
+    re_ref,
+    im_ref,
+    ere_ref,
+    eim_ref,
+    operand_sem,
+    send_sem,
+    recv_sem,
+    extra_send,
+    extra_recv,
+    out_send,
+    out_recv,
+):
+    total_devices = nx * ny
+    depth = ny // 2
+    members = nx * depth
+    chunks = state.shape[0]
+    my_x, my_y = lax.axis_index("sx"), lax.axis_index("sy")
+    my_half = my_y // depth
+    my_place = my_x * depth + lax.rem(my_y, depth)
+    me = my_x * ny + my_y
+    rows = src.shape[0]
+    terms = rows // 2
+    side = out.shape[1]
+
+    def box_of(far, place):
+        half = my_half + far - 2 * my_half * far
+        return place // depth * ny + half * depth + lax.rem(place, depth)
+
+    def coordinates(box):
+        return box // ny, lax.rem(box, ny)
+
+    def lanes_of(place, chunk):
+        return pl.ds(pl.multiple_of((place * chunks + chunk) * LANES, LANES), LANES)
+
+    barrier = pltpu.get_barrier_semaphore()
+
+    @pl.loop(1, total_devices)
+    def _(step):
+        peer = lax.rem(me + step, total_devices)
+        pl.semaphore_signal(barrier, inc=1, device_id=coordinates(peer), device_id_type=MESH)
+
+    loads = [
+        pltpu.make_async_copy(hbm, ref, operand_sem.at[number])
+        for number, (hbm, ref) in enumerate(
+            [(re_hbm, re_ref), (im_hbm, im_ref), (ere_hbm, ere_ref), (eim_hbm, eim_ref)]
+        )
+    ]
+    for load in loads:
+        load.start()
+    for chunk in range(chunks):
+        pltpu.make_async_copy(
+            src.at[:, lanes_of(my_place, chunk)],
+            state.at[chunk, my_place],
+            recv_sem.at[chunk, my_place],
+        ).start()
+    pltpu.make_async_copy(extra.at[my_place], extras.at[me], extra_recv.at[me]).start()
+    picture[...] = jnp.zeros_like(picture)
+
+    pl.semaphore_wait(barrier, total_devices - 1)
+
+    sends = []
+    for chunk in range(chunks):
+        for mask in range(1, members):
+            place = flipped(my_place, mask, members)
+            copy = pltpu.make_async_remote_copy(
+                src_ref=src.at[:, lanes_of(place, chunk)],
+                dst_ref=state.at[chunk, my_place],
+                send_sem=send_sem.at[chunk, mask],
+                recv_sem=recv_sem.at[chunk, my_place],
+                device_id=coordinates(box_of(0, place)),
+                device_id_type=MESH,
+            )
+            copy.start()
+            sends.append(copy)
+        if chunk:
+            continue
+        for far in range(2):
+            for mask in range(1 - far, members):
+                place = flipped(my_place, mask, members)
+                copy = pltpu.make_async_remote_copy(
+                    src_ref=extra.at[place],
+                    dst_ref=extras.at[me],
+                    send_sem=extra_send.at[far, mask],
+                    recv_sem=extra_recv.at[me],
+                    device_id=coordinates(box_of(far, place)),
+                    device_id_type=MESH,
+                )
+                copy.start()
+                sends.append(copy)
+
+    for load in loads:
+        load.wait()
+
+    def put_matrix(target, top, left, level, bit, term):
+        real = re_ref[level, bit, term]
+        imag = im_ref[level, bit, term]
+        target[top : top + terms, left : left + terms] = real
+        target[top : top + terms, left + terms : left + rows] = -imag
+        target[top + terms : top + rows, left : left + terms] = imag
+        target[top + terms : top + rows, left + terms : left + rows] = real
+
+    for level in range(LEVELS):
+        if level == 1:
+            put_matrix(split_mats, 0, 0, level, my_half, 0)
+            put_matrix(split_mats, rows, 0, level, 1 - my_half, 1)
+            continue
+        for bit in range(2):
+            put_matrix(mats.at[level], bit * rows, bit * rows, level, bit, 0)
+            put_matrix(mats.at[level], bit * rows, (1 - bit) * rows, level, bit, 1)
+    evaluate = jnp.concatenate([ere_ref[...], -eim_ref[...]], axis=1)
+
+    @pl.loop(0, total_devices)
+    def _(box):
+        pltpu.make_async_copy(extras.at[box], extras.at[box], extra_recv.at[box]).wait()
+        for chunk in range(chunks):
+            cosine = extras[box, :, chunk * LANES : (chunk + 1) * LANES]
+            sine = extras[box, :, (chunks + chunk) * LANES : (chunks + chunk + 1) * LANES]
+            real, imag = cosine, sine
+            for level in range(LEVELS):
+                rotors[chunk, level, 0, box] = real
+                rotors[chunk, level, 1, box] = imag
+                if level + 1 < LEVELS:
+                    real, imag = real * cosine - imag * sine, real * sine + imag * cosine
+
+    def turned(piece, chunk, level, box):
+        real, imag = piece[:terms], piece[terms:]
+        cosine = rotors[chunk, level, 0, box]
+        sine = rotors[chunk, level, 1, box]
+        new_real = (cosine * real - sine * imag).astype(jnp.bfloat16)
+        new_imag = (sine * real + cosine * imag).astype(jnp.bfloat16)
+        return new_real, new_imag
+
+    def pairs_of(group, level):
+        axis_size = nx if level % 2 == 0 else ny
+        stride = (depth if level % 2 == 0 else 1) << (axis_size.bit_length() - 2 - level // 2)
+        found = []
+        for part in range(2):
+            pair = 2 * group + part
+            low = pair // stride * (2 * stride) + lax.rem(pair, stride)
+            found.append((low, low + stride))
+        return found
+
+    def exchange(boxes_ref, chunk, level, far, group):
+        pairs = pairs_of(group, level)
+        stacked = jnp.concatenate(
+            [jnp.concatenate([boxes_ref[low], boxes_ref[high]], axis=0) for low, high in pairs],
+            axis=1,
+        )
+        sums = jnp.dot(mats[level], stacked, preferred_element_type=jnp.float32)
+        for part, pair in enumerate(pairs):
+            for bit, place in enumerate(pair):
+                piece = sums[bit * rows : (bit + 1) * rows, part * LANES : (part + 1) * LANES]
+                real, imag = turned(piece, chunk, level, box_of(far, place))
+                boxes_ref[place, 0:terms] = real
+                boxes_ref[place, terms:rows] = imag
+
+    @pl.loop(0, chunks)
+    def _(chunk):
+        @pl.loop(0, members)
+        def _(place):
+            block = state.at[chunk, place]
+            pltpu.make_async_copy(block, block, recv_sem.at[chunk, place]).wait()
+
+        def first(group, _):
+            exchange(state.at[chunk], chunk, 0, 0, group)
+            return 0
+
+        lax.fori_loop(0, members // 4, first, 0, unroll=UNROLL)
+
+        def second(group, _):
+            places = [2 * group, 2 * group + 1]
+            stacked = jnp.concatenate([state[chunk, place] for place in places], axis=1)
+            sums = jnp.dot(split_mats[...], stacked, preferred_element_type=jnp.float32)
+            for part, place in enumerate(places):
+                for far in range(2):
+                    piece = sums[far * rows : (far + 1) * rows, part * LANES : (part + 1) * LANES]
+                    real, imag = turned(piece, chunk, 1, box_of(far, place))
+                    partial[far, place, 0:terms] = real
+                    partial[far, place, terms:rows] = imag
+            return 0
+
+        lax.fori_loop(0, members // 2, second, 0, unroll=UNROLL)
+
+        for level in range(2, LEVELS):
+
+            def later(step, _, level=level):
+                for far in range(2):
+                    exchange(partial.at[far], chunk, level, far, step)
+                return 0
+
+            lax.fori_loop(0, members // 4, later, 0, unroll=UNROLL)
+
+        def render(place, _):
+            stacked = jnp.concatenate([partial[0, place], partial[1, place]], axis=1)
+            cells = jnp.dot(evaluate, stacked, preferred_element_type=jnp.float32)
+            for far in range(2):
+                block = cells[:, far * LANES : (far + 1) * LANES].reshape(side, side, LANES)
+                row, col = coordinates(box_of(far, place))
+                picture[pl.ds(row * side + 2, side), col + 1] = block
+            return 0
+
+        lax.fori_loop(0, members, render, 0, unroll=UNROLL)
+
+        def smooth(far, place):
+            box = box_of(far, place)
+            row, col = coordinates(box)
+            values = picture[pl.ds(row * side, side + 4), pl.ds(col, 3)]
+            rows_near = values[1:-3] + values[2:-2] + values[3:-1]
+            rows_far = rows_near + values[0:-4] + values[4:]
+            rows_near = rows_near.reshape(side, 3 * side, LANES)
+            rows_far = rows_far.reshape(side, 3 * side, LANES)
+
+            def moved(block, shift):
+                return block[:, side + shift : 2 * side + shift]
+
+            box_near = moved(rows_near, -1) + moved(rows_near, 0) + moved(rows_near, 1)
+            box_far = (
+                moved(rows_far, -1)
+                + moved(rows_far, 0)
+                + moved(rows_far, 1)
+                + moved(rows_far, -2)
+                + moved(rows_far, 2)
+            )
+            wide = extras[box, :, 2 * chunks * LANES :].reshape(1, 1, LANES) == 2.0
+            chosen = jnp.where(wide, box_far / 25.0, box_near / 9.0)
+            tiles[chunk, far, place] = chosen.astype(jnp.bfloat16)
+
+        for far in (1, 0):
+            for mask in range(members):
+                place = flipped(my_place, mask, members)
+                smooth(far, place)
+                source = tiles.at[chunk, far, place]
+                target = out.at[far, :, :, lanes_of(my_place, chunk)]
+                arrived = out_recv.at[chunk, far, my_place]
+                if far == 0 and mask == 0:
+                    pltpu.make_async_copy(source, target, arrived).start()
+                else:
+                    pltpu.make_async_remote_copy(
+                        src_ref=source,
+                        dst_ref=target,
+                        send_sem=out_send.at[chunk, far, mask],
+                        recv_sem=arrived,
+                        device_id=coordinates(box_of(far, place)),
+                        device_id_type=MESH,
+                    ).start()
+
+    for copy in sends:
+        copy.wait_send()
+
+    for far in range(2):
+        for chunk in range(chunks):
+
+            @pl.loop(1 - far, members)
+            def _(mask, far=far, chunk=chunk):
+                block = tiles.at[chunk, far, mask]
+                pltpu.make_async_copy(block, block, out_send.at[chunk, far, mask]).wait()
+
+            @pl.loop(0, members)
+            def _(place, far=far, chunk=chunk):
+                block = tiles.at[chunk, far, place]
+                pltpu.make_async_copy(block, block, out_recv.at[chunk, far, place]).wait()
+
+
+def spread_on_device(
+    nx,
+    ny,
+    sources,
+    translate_re,
+    translate_im,
+    frame_index,
+    velocity_index,
+    eval_re,
+    eval_im,
+    window,
+):
+    total_devices = nx * ny
+    members = total_devices // 2
+    terms, columns = sources.shape[3:]
+    rows = 2 * terms
+    side = math.isqrt(eval_re.shape[0])
+    share = columns // members
+    chunks = share // LANES
+    product = frame_index[0, 0][:, None] * velocity_index[0, 0][None, :] % VGRID
+    angles = (TWO_PI / VGRID * product.astype(jnp.float32)).reshape(members, 1, share)
+    widths = jnp.broadcast_to(window[0, 0].astype(jnp.float32), (members, 1, LANES))
+    extra = jnp.concatenate([jnp.cos(angles), jnp.sin(angles), widths], axis=-1)
+    anywhere = pl.BlockSpec(memory_space=pl.ANY)
+    dma = pltpu.SemaphoreType.DMA
+    halves = pl.pallas_call(
+        functools.partial(spread_kernel, nx, ny),
+        out_shape=jax.ShapeDtypeStruct((2, side, side, columns), jnp.bfloat16),
+        in_specs=[anywhere] * 6,
+        out_specs=anywhere,
+        scratch_shapes=[
+            pltpu.VMEM((chunks, members, rows, LANES), jnp.bfloat16),
+            pltpu.VMEM((2, members, rows, LANES), jnp.bfloat16),
+            pltpu.VMEM((total_devices, 1, 2 * share + LANES), jnp.float32),
+            pltpu.VMEM((LEVELS, 2 * rows, 2 * rows), jnp.bfloat16),
+            pltpu.VMEM((2 * rows, rows), jnp.bfloat16),
+            pltpu.VMEM((nx * side + 4, ny + 2, side, LANES), jnp.float32),
+            pltpu.VMEM((chunks, 2, members, side, side, LANES), jnp.bfloat16),
+            pltpu.VMEM((chunks, LEVELS, 2, total_devices, 1, LANES), jnp.float32),
+            pltpu.VMEM(translate_re.shape, jnp.bfloat16),
+            pltpu.VMEM(translate_im.shape, jnp.bfloat16),
+            pltpu.VMEM(eval_re.shape, jnp.bfloat16),
+            pltpu.VMEM(eval_im.shape, jnp.bfloat16),
+            dma((4,)),
+            dma((chunks, members)),
+            dma((chunks, members)),
+            dma((2, members)),
+            dma((total_devices,)),
+            dma((chunks, 2, members)),
+            dma((chunks, 2, members)),
+        ],
+        compiler_params=pltpu.CompilerParams(collective_id=0, has_side_effects=True),
+    )(
+        sources[0, 0].reshape(rows, columns),
+        extra,
+        translate_re,
+        translate_im,
+        eval_re,
+        eval_im,
+    )
+    return (halves[0].astype(jnp.float32) + halves[1].astype(jnp.float32)).astype(jnp.bfloat16)
+
+
 def solution(mesh):
+    nx, ny = mesh.shape["sx"], mesh.shape["sy"]
+
+    def body(sources, *others):
+        members = nx * ny // 2
+        if sources.shape[4] % (members * LANES) == 0:
+            return spread_on_device(nx, ny, sources, *others)
+        return on_device(sources, *others)
+
     return jax.shard_map(
-        on_device,
+        body,
         mesh=mesh,
         in_specs=(
             P("sx", "sy", None, None, None),

time: 153 us -> 55.5 us (0.36)
  the two profiles are of different devices: /device:TPU:20 before, /device:TPU:0 now
where the time goes in v2:
time: 55.5 us; the launch traced here: 55.3 us
  Pallas kernels  50.6 us (91%)
  other arithmetic  3.31 us (6%)
  between operations  0.7 us (1%)
  local copies, waits for them, and re-layouts  0.66 us (1%)
    pallas_call x1, Pallas kernels, spread_on_device(): pl.pallas_call(functools.partial(spread_kernel, nx, ny), out_shape=jax.Sh...  50.6 us
    convert_element_type x1, other arithmetic, spread_on_device(): (halves[0].astype(jnp.float32) + halves[1].astype(jnp.float32)).astype(jn...  2.12 us

profile of v2, /device:TPU:0, one launch (start us, length us, event | category | flops | bytes accessed | tf_op | source)
XLA Modules:
  0.0 55.3 jit_solution(3026914200846857243)
XLA Ops:
  0.7 0.0 copy-start
  0.7 0.0 copy-start.1
  0.7 0.6 %copy-done = s32[1,1,256]{2,1,0:T(1,128)S(1)} copy-done((s32[1,1,256]{2,1,0:T(1,128)S(1)}, s32[1,1,256]{2,1,0:T(1,128)}, u32[]{:S(2)}) %copy-start) | copy-done | bytes 1048
  1.3 0.0 copy-done.1
  1.3 0.1 fusion.1
  1.4 0.5 fusion.4
  1.9 0.7 %maximum_maximum_fusion.extra = f32[16,1,640]{2,1,0:T(1,128)} fusion(f32[16,1,256]{2,1,0:T(1,128)S(1)} %get-tuple-element.6, f32[16,1,256]{2,1,0:T(1,128)S(1)} %get-tuple-element.5, f32[640]{0:T(1024)S(1)} %pad.2.clone), kind=kLoop, calls=%fused_computation.2 | loop fusion | flops 20480 | bytes 76288 | tf_op jit(solution)/shard_map/concatenate | solution.py:417
  2.6 50.6 %shard_map.82 = bf16[2,8,8,4096]{3,2,1,0:T(8,128)(2,1)} custom-call(bf16[128,4096]{1,0:T(8,128)(2,1)} %bitcast.6, f32[16,1,640]{2,1,0:T(1,128)} %maximum_maximum_fusion.extra, bf16[4,2,2,64,64]{4,3,2,1,0:T(8,128)(2,1)} %re_hbm.1, bf16[4,2,2,64,64]{4,3,2,1,0:T(8,128)(2,1)} %im_hbm.1, bf16[64,64]{1,0:T(8,128)(2,1)} %ere_hbm.1, bf16[64,64]{1,0:T(8,128)(2,1)} %eim_hbm.1), custom_call_target="tpu_custom_call" | custom-call | tf_op jit(solution)/shard_map/pallas_call | solution.py:420
  53.2 2.1 %fusion = bf16[8,8,4096]{2,1,0:T(8,128)(2,1)} fusion(bf16[2,8,8,4096]{3,2,1,0:T(8,128)(2,1)} %shard_map.82), kind=kLoop, calls=%fused_computation.1 | loop fusion | flops 1048576 | bytes 1572864 | tf_op jit(solution)/shard_map/convert_element_type | solution.py:455
  (2 shorter events, 0.0 us)
Async XLA Ops:
  0.7 0.7 %copy-start = (s32[1,1,256]{2,1,0:T(1,128)S(1)}, s32[1,1,256]{2,1,0:T(1,128)}, u32[]{:S(2)}) copy-start(s32[1,1,256]{2,1,0:T(1,128)} %param.12) | copy-start | bytes 3076
  0.7 0.7 %copy-start.1 = (s32[1,1,16]{2,1,0:T(1,128)S(1)}, s32[1,1,16]{2,1,0:T(1,128)}, u32[]{:S(2)}) copy-start(s32[1,1,16]{2,1,0:T(1,128)} %param.11) | copy-start | bytes 196

commit v3 on v0

--- a/solution.py
+++ b/solution.py
@@ -1,8 +1,11 @@
+import functools
 import math
 
 import jax
 import jax.numpy as jnp
 from jax import lax
+from jax.experimental import pallas as pl
+from jax.experimental.pallas import tpu as pltpu
 from jax.sharding import PartitionSpec as P
 
 LEVELS = 4
@@ -94,9 +97,460 @@
     return chosen.astype(jnp.bfloat16)
 
 
+MESH = pl.DeviceIdType.MESH
+LANES = 128
+UNROLL = 4
+
+
+def flipped(index, mask, total):
+    bit = 1
+    while bit < total:
+        if mask & bit:
+            index = index + bit - 2 * bit * (index // bit % 2)
+        bit *= 2
+    return index
+
+
+def spread_kernel(
+    nx,
+    ny,
+    src,
+    extra,
+    re_hbm,
+    im_hbm,
+    ere_hbm,
+    eim_hbm,
+    out,
+    other,
+    state,
+    whole,
+    partial,
+    extras,
+    mats,
+    split_mats,
+    picture,
+    tiles,
+    whole_tiles,
+    rotors,
+    re_ref,
+    im_ref,
+    ere_ref,
+    eim_ref,
+    operand_sem,
+    send_sem,
+    recv_sem,
+    whole_send,
+    whole_recv,
+    extra_send,
+    extra_recv,
+    out_send,
+    out_recv,
+    whole_out_send,
+    whole_out_recv,
+):
+    total_devices = nx * ny
+    depth = ny // 2
+    members = nx * depth
+    my_x, my_y = lax.axis_index("sx"), lax.axis_index("sy")
+    my_half = my_y // depth
+    my_place = my_x * depth + lax.rem(my_y, depth)
+    me = my_x * ny + my_y
+    my_seat = my_x // 2 * ny + my_y
+    seated = lax.rem(my_x, 2) == 0
+    rows = src.shape[0]
+    terms = rows // 2
+    side = out.shape[0]
+
+    def box_of(far, place):
+        half = my_half + far - 2 * my_half * far
+        return place // depth * ny + half * depth + lax.rem(place, depth)
+
+    def coordinates(box):
+        return box // ny, lax.rem(box, ny)
+
+    def box_at(seat):
+        return seat // ny * 2 * ny + lax.rem(seat, ny)
+
+    def lanes_of(number):
+        return pl.ds(pl.multiple_of(number * LANES, LANES), LANES)
+
+    barrier = pltpu.get_barrier_semaphore()
+
+    @pl.loop(1, total_devices)
+    def _(step):
+        peer = lax.rem(me + step, total_devices)
+        pl.semaphore_signal(barrier, inc=1, device_id=coordinates(peer), device_id_type=MESH)
+
+    loads = [
+        pltpu.make_async_copy(hbm, ref, operand_sem.at[number])
+        for number, (hbm, ref) in enumerate(
+            [(re_hbm, re_ref), (im_hbm, im_ref), (ere_hbm, ere_ref), (eim_hbm, eim_ref)]
+        )
+    ]
+    for load in loads:
+        load.start()
+    pltpu.make_async_copy(
+        src.at[:, lanes_of(my_place)], state.at[my_place], recv_sem.at[my_place]
+    ).start()
+    pltpu.make_async_copy(extra.at[my_place], extras.at[0, me], extra_recv.at[0, me]).start()
+
+    @pl.when(seated)
+    def _():
+        number = members + my_seat
+        pltpu.make_async_copy(
+            src.at[:, lanes_of(number)], whole.at[me], whole_recv.at[me]
+        ).start()
+        pltpu.make_async_copy(extra.at[number], extras.at[1, me], extra_recv.at[1, me]).start()
+
+    picture[...] = jnp.zeros_like(picture)
+
+    pl.semaphore_wait(barrier, total_devices - 1)
+
+    def send(source, target, sent, arrived, box):
+        copy = pltpu.make_async_remote_copy(
+            src_ref=source,
+            dst_ref=target,
+            send_sem=sent,
+            recv_sem=arrived,
+            device_id=coordinates(box),
+            device_id_type=MESH,
+        )
+        copy.start()
+        return copy
+
+    sends = []
+    for mask in range(1, members):
+        place = flipped(my_place, mask, members)
+        sends.append(
+            send(
+                src.at[:, lanes_of(place)],
+                state.at[my_place],
+                send_sem.at[mask],
+                recv_sem.at[my_place],
+                box_of(0, place),
+            )
+        )
+    for far in range(2):
+        for mask in range(1 - far, members):
+            place = flipped(my_place, mask, members)
+            sends.append(
+                send(
+                    extra.at[place],
+                    extras.at[0, me],
+                    extra_send.at[far, mask],
+                    extra_recv.at[0, me],
+                    box_of(far, place),
+                )
+            )
+
+    def send_whole(mask):
+        seat = flipped(my_seat, mask, members)
+        number = members + seat
+        return [
+            send(
+                src.at[:, lanes_of(number)],
+                whole.at[me],
+                whole_send.at[mask],
+                whole_recv.at[me],
+                box_at(seat),
+            ),
+            send(
+                extra.at[number],
+                extras.at[1, me],
+                extra_send.at[2, mask],
+                extra_recv.at[1, me],
+                box_at(seat),
+            ),
+        ]
+
+    half_mask = ny // 2
+    for mask in sorted(range(1, members), key=lambda mask: (0 if mask & half_mask else 1, mask)):
+        sends += send_whole(mask)
+
+    @pl.when(jnp.logical_not(seated))
+    def _():
+        for copy in send_whole(0):
+            copy.wait_send()
+
+    for load in loads:
+        load.wait()
+
+    def put_matrix(target, top, left, level, bit, term):
+        real = re_ref[level, bit, term]
+        imag = im_ref[level, bit, term]
+        target[top : top + terms, left : left + terms] = real
+        target[top : top + terms, left + terms : left + rows] = -imag
+        target[top + terms : top + rows, left : left + terms] = imag
+        target[top + terms : top + rows, left + terms : left + rows] = real
+
+    for level in range(LEVELS):
+        if level == 1:
+            put_matrix(split_mats, 0, 0, level, my_half, 0)
+            put_matrix(split_mats, rows, 0, level, 1 - my_half, 1)
+        for bit in range(2):
+            put_matrix(mats.at[level], bit * rows, bit * rows, level, bit, 0)
+            put_matrix(mats.at[level], bit * rows, (1 - bit) * rows, level, bit, 1)
+    evaluate = jnp.concatenate([ere_ref[...], -eim_ref[...]], axis=1)
+
+    def collect_rotors(kind):
+        @pl.loop(0, total_devices)
+        def _(box):
+            block = extras.at[kind, box]
+            pltpu.make_async_copy(block, block, extra_recv.at[kind, box]).wait()
+            cosine = extras[kind, box, :, 0:LANES]
+            sine = extras[kind, box, :, LANES : 2 * LANES]
+            real, imag = cosine, sine
+            for level in range(LEVELS):
+                rotors[kind, level, 0, box] = real
+                rotors[kind, level, 1, box] = imag
+                if level + 1 < LEVELS:
+                    real, imag = real * cosine - imag * sine, real * sine + imag * cosine
+
+    def turned(piece, chunk, level, box):
+        real, imag = piece[:terms], piece[terms:]
+        cosine = rotors[chunk, level, 0, box]
+        sine = rotors[chunk, level, 1, box]
+        new_real = (cosine * real - sine * imag).astype(jnp.bfloat16)
+        new_imag = (sine * real + cosine * imag).astype(jnp.bfloat16)
+        return new_real, new_imag
+
+    def exchange(boxes_ref, kind, level, box_at_index, width, group):
+        axis_size = nx if level % 2 == 0 else ny
+        stride = (width if level % 2 == 0 else 1) << (axis_size.bit_length() - 2 - level // 2)
+        pairs = []
+        for part in range(2):
+            pair = 2 * group + part
+            low = pair // stride * (2 * stride) + lax.rem(pair, stride)
+            pairs.append((low, low + stride))
+        stacked = jnp.concatenate(
+            [jnp.concatenate([boxes_ref[low], boxes_ref[high]], axis=0) for low, high in pairs],
+            axis=1,
+        )
+        sums = jnp.dot(mats[level], stacked, preferred_element_type=jnp.float32)
+        for part, pair in enumerate(pairs):
+            for bit, index in enumerate(pair):
+                piece = sums[bit * rows : (bit + 1) * rows, part * LANES : (part + 1) * LANES]
+                real, imag = turned(piece, kind, level, box_at_index(index))
+                boxes_ref[index, 0:terms] = real
+                boxes_ref[index, terms:rows] = imag
+
+    def render(states, boxes):
+        stacked = jnp.concatenate(states, axis=1)
+        cells = jnp.dot(evaluate, stacked, preferred_element_type=jnp.float32)
+        for part, box in enumerate(boxes):
+            block = cells[:, part * LANES : (part + 1) * LANES].reshape(side, side, LANES)
+            row, col = coordinates(box)
+            picture[pl.ds(row * side + 2, side), col + 1] = block
+
+    def smooth(box):
+        row, col = coordinates(box)
+        values = picture[pl.ds(row * side, side + 4), pl.ds(col, 3)]
+        rows_near = values[1:-3] + values[2:-2] + values[3:-1]
+        rows_far = rows_near + values[0:-4] + values[4:]
+        rows_near = rows_near.reshape(side, 3 * side, LANES)
+        rows_far = rows_far.reshape(side, 3 * side, LANES)
+
+        def moved(block, shift):
+            return block[:, side + shift : 2 * side + shift]
+
+        box_near = moved(rows_near, -1) + moved(rows_near, 0) + moved(rows_near, 1)
+        box_far = (
+            moved(rows_far, -1)
+            + moved(rows_far, 0)
+            + moved(rows_far, 1)
+            + moved(rows_far, -2)
+            + moved(rows_far, 2)
+        )
+        wide = extras[0, box, :, 2 * LANES :].reshape(1, 1, LANES) == 2.0
+        return jnp.where(wide, box_far / 25.0, box_near / 9.0).astype(jnp.bfloat16)
+
+    def repeat(count, step):
+        def body(index, _):
+            step(index)
+            return 0
+
+        lax.fori_loop(0, count, body, 0, unroll=UNROLL)
+
+    collect_rotors(0)
+
+    @pl.loop(0, members)
+    def _(place):
+        block = state.at[place]
+        pltpu.make_async_copy(block, block, recv_sem.at[place]).wait()
+
+    repeat(
+        members // 4, lambda group: exchange(state, 0, 0, lambda i: box_of(0, i), depth, group)
+    )
+
+    def split(group):
+        places = [2 * group, 2 * group + 1]
+        stacked = jnp.concatenate([state[place] for place in places], axis=1)
+        sums = jnp.dot(split_mats[...], stacked, preferred_element_type=jnp.float32)
+        for part, place in enumerate(places):
+            for far in range(2):
+                piece = sums[far * rows : (far + 1) * rows, part * LANES : (part + 1) * LANES]
+                real, imag = turned(piece, 0, 1, box_of(far, place))
+                partial[far, place, 0:terms] = real
+                partial[far, place, terms:rows] = imag
+
+    repeat(members // 2, split)
+    for level in range(2, LEVELS):
+
+        def later(group, level=level):
+            for far in range(2):
+                exchange(partial.at[far], 0, level, lambda i: box_of(far, i), depth, group)
+
+        repeat(members // 4, later)
+    repeat(
+        members,
+        lambda place: render(
+            [partial[0, place], partial[1, place]], [box_of(0, place), box_of(1, place)]
+        ),
+    )
+    for far in (1, 0):
+        target = (other if far else out).at[:, :, lanes_of(my_place)]
+        arrived = out_recv.at[far, my_place]
+        for mask in range(members):
+            place = flipped(my_place, mask, members)
+            source = tiles.at[far, place]
+            tiles[far, place] = smooth(box_of(far, place))
+            if far == 0 and mask == 0:
+                pltpu.make_async_copy(source, target, arrived).start()
+            else:
+                sent = out_send.at[far, mask]
+                sends.append(send(source, target, sent, arrived, box_of(far, place)))
+
+    @pl.when(seated)
+    def _():
+        collect_rotors(1)
+
+        @pl.loop(0, total_devices)
+        def _(box):
+            block = whole.at[box]
+            pltpu.make_async_copy(block, block, whole_recv.at[box]).wait()
+
+        for level in range(LEVELS):
+            repeat(
+                total_devices // 4,
+                lambda group, level=level: exchange(whole, 1, level, lambda i: i, ny, group),
+            )
+        repeat(
+            total_devices // 2,
+            lambda group: render(
+                [whole[2 * group], whole[2 * group + 1]], [2 * group, 2 * group + 1]
+            ),
+        )
+        target = out.at[:, :, lanes_of(members + my_seat)]
+        arrived = whole_out_recv.at[my_seat]
+        finals = []
+        order = sorted(
+            range(1, total_devices), key=lambda mask: (0 if mask & half_mask else 1, mask)
+        )
+        for mask in order:
+            box = flipped(me, mask, total_devices)
+            whole_tiles[box] = smooth(box).astype(jnp.bfloat16)
+            sent = whole_out_send.at[mask]
+            finals.append(send(whole_tiles.at[box], target, sent, arrived, box))
+        whole_tiles[me] = smooth(me)
+        pltpu.make_async_copy(whole_tiles.at[me], target, arrived).start()
+        for copy in finals:
+            copy.wait_send()
+
+    for copy in sends:
+        copy.wait_send()
+
+    @pl.loop(0, members)
+    def _(place):
+        for far in range(2):
+            block = tiles.at[far, place]
+            pltpu.make_async_copy(block, block, out_recv.at[far, place]).wait()
+        block = whole_tiles.at[place]
+        pltpu.make_async_copy(block, block, whole_out_recv.at[place]).wait()
+
+
+def spread_on_device(
+    nx,
+    ny,
+    sources,
+    translate_re,
+    translate_im,
+    frame_index,
+    velocity_index,
+    eval_re,
+    eval_im,
+    window,
+):
+    total_devices = nx * ny
+    members = total_devices // 2
+    terms, columns = sources.shape[3:]
+    rows = 2 * terms
+    side = math.isqrt(eval_re.shape[0])
+    slabs = columns // LANES
+    product = frame_index[0, 0][:, None] * velocity_index[0, 0][None, :] % VGRID
+    angles = (TWO_PI / VGRID * product.astype(jnp.float32)).reshape(slabs, 1, LANES)
+    widths = jnp.broadcast_to(window[0, 0].astype(jnp.float32), angles.shape)
+    extra = jnp.concatenate([jnp.cos(angles), jnp.sin(angles), widths], axis=-1)
+    anywhere = pl.BlockSpec(memory_space=pl.ANY)
+    dma = pltpu.SemaphoreType.DMA
+    vmem = pltpu.VMEM
+    out, other = pl.pallas_call(
+        functools.partial(spread_kernel, nx, ny),
+        out_shape=(
+            jax.ShapeDtypeStruct((side, side, columns), jnp.bfloat16),
+            jax.ShapeDtypeStruct((side, side, members * LANES), jnp.bfloat16),
+        ),
+        in_specs=[anywhere] * 6,
+        out_specs=(anywhere, anywhere),
+        scratch_shapes=[
+            vmem((members, rows, LANES), jnp.bfloat16),
+            vmem((total_devices, rows, LANES), jnp.bfloat16),
+            vmem((2, members, rows, LANES), jnp.bfloat16),
+            vmem((2, total_devices, 1, 3 * LANES), jnp.float32),
+            vmem((LEVELS, 2 * rows, 2 * rows), jnp.bfloat16),
+            vmem((2 * rows, rows), jnp.bfloat16),
+            vmem((nx * side + 4, ny + 2, side, LANES), jnp.float32),
+            vmem((2, members, side, side, LANES), jnp.bfloat16),
+            vmem((total_devices, side, side, LANES), jnp.bfloat16),
+            vmem((2, LEVELS, 2, total_devices, 1, LANES), jnp.float32),
+            vmem(translate_re.shape, jnp.bfloat16),
+            vmem(translate_im.shape, jnp.bfloat16),
+            vmem(eval_re.shape, jnp.bfloat16),
+            vmem(eval_im.shape, jnp.bfloat16),
+            dma((4,)),
+            dma((members,)),
+            dma((members,)),
+            dma((members,)),
+            dma((total_devices,)),
+            dma((3, members)),
+            dma((2, total_devices)),
+            dma((2, members)),
+            dma((2, members)),
+            dma((total_devices,)),
+            dma((members,)),
+        ],
+        compiler_params=pltpu.CompilerParams(collective_id=0, has_side_effects=True),
+    )(
+        sources[0, 0].reshape(rows, columns),
+        extra,
+        translate_re,
+        translate_im,
+        eval_re,
+        eval_im,
+    )
+    other = jnp.pad(other, ((0, 0), (0, 0), (0, columns - other.shape[2])))
+    return (out.astype(jnp.float32) + other.astype(jnp.float32)).astype(jnp.bfloat16)
+
+
 def solution(mesh):
+    nx, ny = mesh.shape["sx"], mesh.shape["sy"]
+
+    def body(sources, *others):
+        if sources.shape[4] == nx * ny * LANES:
+            return spread_on_device(nx, ny, sources, *others)
+        return on_device(sources, *others)
+
     return jax.shard_map(
-        on_device,
+        body,
         mesh=mesh,
         in_specs=(
             P("sx", "sy", None, None, None),

time: 153 us -> 48.7 us (0.32)
  the two profiles are of different devices: /device:TPU:20 before, /device:TPU:0 now
where the time goes in v3:
time: 48.7 us; the launch traced here: 48.4 us
  Pallas kernels  43.1 us (89%)
  other arithmetic  3.18 us (7%)
  local copies, waits for them, and re-layouts  1.4 us (3%)
  between operations  0.7 us (1%)
    pallas_call x1, Pallas kernels, spread_on_device(): pl.pallas_call(functools.partial(spread_kernel, nx, ny), out_shape=(jax.S...  43.1 us
    convert_element_type x1, other arithmetic, spread_on_device(): (out.astype(jnp.float32) + other.astype(jnp.float32)).astype(jnp.bfloat16)  1.97 us
    unnamed x4, local copies, waits for them, and re-layouts  1.23 us

profile of v3, /device:TPU:0, one launch (start us, length us, event | category | flops | bytes accessed | tf_op | source)
XLA Modules:
  0.0 48.4 jit_solution(11553480894365888836)
XLA Ops:
  0.7 0.0 copy-start.1
  0.7 0.6 %copy-done.1 = s32[1,1,16]{2,1,0:T(1,128)S(1)} copy-done((s32[1,1,16]{2,1,0:T(1,128)S(1)}, s32[1,1,16]{2,1,0:T(1,128)}, u32[]{:S(2)}) %copy-start.1) | copy-done | bytes 88
  1.3 0.1 mul.56
  1.4 0.0 copy-start
  1.4 0.1 mul.57
  1.5 0.6 %copy-done = s32[1,1,256]{2,1,0:T(1,128)S(1)} copy-done((s32[1,1,256]{2,1,0:T(1,128)S(1)}, s32[1,1,256]{2,1,0:T(1,128)}, u32[]{:S(2)}) %copy-start) | copy-done | bytes 1048
  2.1 0.1 fusion.1
  2.2 0.5 multiply_cosine_fusion
  2.6 0.7 %maximum_maximum_fusion.extra = f32[32,1,384]{2,1,0:T(1,128)} fusion(f32[32,1,128]{2,1,0:T(1,128)S(1)} %get-tuple-element.10, f32[32,1,128]{2,1,0:T(1,128)S(1)} %get-tuple-element.9, f32[384]{0:T(512)S(1)} %pad.7.clone), kind=kLoop, calls=%fused_computation.1 | loop fusion | flops 24576 | bytes 83456 | tf_op jit(solution)/shard_map/concatenate | solution.py:492
  3.3 43.1 %shard_map.82 = (bf16[8,8,4096]{2,1,0:T(8,128)(2,1)}, bf16[8,8,2048]{2,1,0:T(8,128)(2,1)}) custom-call(bf16[128,4096]{1,0:T(8,128)(2,1)} %bitcast.6, f32[32,1,384]{2,1,0:T(1,128)} %maximum_maximum_fusion.extra, bf16[4,2,2,64,64]{4,3,2,1,0:T(8,128)(2,1)} %re_hbm.1, bf16[4,2,2,64,64]{4,3,2,1,0:T(8,128)(2,1)} %im_hbm.1, bf16[64,64]{1,0:T(8,128)(2,1)} %ere_hbm.1, ...), custom_call_target="tpu_custom_call" | custom-call | tf_op jit(solution)/shard_map/pallas_call | solution.py:496
  46.4 2.0 %add_convert_fusion = bf16[8,8,4096]{2,1,0:T(8,128)(2,1)} fusion(bf16[8,8,4096]{2,1,0:T(8,128)(2,1)} %get-tuple-element.7, bf16[8,8,2048]{2,1,0:T(8,128)(2,1)} %get-tuple-element.8), kind=kLoop, calls=%fused_computation | loop fusion | flops 1048576 | bytes 1310720 | tf_op jit(solution)/shard_map/convert_element_type | solution.py:541
  (3 shorter events, 0.0 us)
Async XLA Ops:
  0.7 0.7 %copy-start.1 = (s32[1,1,16]{2,1,0:T(1,128)S(1)}, s32[1,1,16]{2,1,0:T(1,128)}, u32[]{:S(2)}) copy-start(s32[1,1,16]{2,1,0:T(1,128)} %param.11) | copy-start | bytes 196
  1.4 0.7 %copy-start = (s32[1,1,256]{2,1,0:T(1,128)S(1)}, s32[1,1,256]{2,1,0:T(1,128)}, u32[]{:S(2)}) copy-start(s32[1,1,256]{2,1,0:T(1,128)} %param.12) | copy-start | bytes 3076

commit v4 on v3

--- a/solution.py
+++ b/solution.py
@@ -115,7 +115,9 @@
     nx,
     ny,
     src,
-    extra,
+    frame_hbm,
+    velocity_hbm,
+    window_hbm,
     re_hbm,
     im_hbm,
     ere_hbm,
@@ -125,7 +127,12 @@
     state,
     whole,
     partial,
+    extra,
     extras,
+    frames,
+    velocities,
+    width,
+    products,
     mats,
     split_mats,
     picture,
@@ -184,11 +191,33 @@
     loads = [
         pltpu.make_async_copy(hbm, ref, operand_sem.at[number])
         for number, (hbm, ref) in enumerate(
-            [(re_hbm, re_ref), (im_hbm, im_ref), (ere_hbm, ere_ref), (eim_hbm, eim_ref)]
+            [
+                (frame_hbm, frames),
+                (velocity_hbm, velocities),
+                (window_hbm, width),
+                (re_hbm, re_ref),
+                (im_hbm, im_ref),
+                (ere_hbm, ere_ref),
+                (eim_hbm, eim_ref),
+            ]
         )
     ]
     for load in loads:
         load.start()
+    for load in loads[:3]:
+        load.wait()
+    points = velocities.shape[2]
+    for number in range(total_devices):
+        frame, offset = divmod(number * LANES, points)
+        speeds = velocities[0, :, offset : offset + LANES]
+        products[number : number + 1] = lax.rem(frames[0, 0, frame] * speeds, VGRID)
+    angles = TWO_PI / VGRID * products[...].astype(jnp.float32)
+    cosines, sines = jnp.cos(angles), jnp.sin(angles)
+    widths = jnp.full((1, LANES), width[0, 0], jnp.int32).astype(jnp.float32)
+    for number in range(total_devices):
+        extra[number, :, 0:LANES] = cosines[number : number + 1]
+        extra[number, :, LANES : 2 * LANES] = sines[number : number + 1]
+        extra[number, :, 2 * LANES :] = widths
     pltpu.make_async_copy(
         src.at[:, lanes_of(my_place)], state.at[my_place], recv_sem.at[my_place]
     ).start()
@@ -272,7 +301,7 @@
         for copy in send_whole(0):
             copy.wait_send()
 
-    for load in loads:
+    for load in loads[3:]:
         load.wait()
 
     def put_matrix(target, top, left, level, bit, term):
@@ -485,11 +514,6 @@
     terms, columns = sources.shape[3:]
     rows = 2 * terms
     side = math.isqrt(eval_re.shape[0])
-    slabs = columns // LANES
-    product = frame_index[0, 0][:, None] * velocity_index[0, 0][None, :] % VGRID
-    angles = (TWO_PI / VGRID * product.astype(jnp.float32)).reshape(slabs, 1, LANES)
-    widths = jnp.broadcast_to(window[0, 0].astype(jnp.float32), angles.shape)
-    extra = jnp.concatenate([jnp.cos(angles), jnp.sin(angles), widths], axis=-1)
     anywhere = pl.BlockSpec(memory_space=pl.ANY)
     dma = pltpu.SemaphoreType.DMA
     vmem = pltpu.VMEM
@@ -499,13 +523,18 @@
             jax.ShapeDtypeStruct((side, side, columns), jnp.bfloat16),
             jax.ShapeDtypeStruct((side, side, members * LANES), jnp.bfloat16),
         ),
-        in_specs=[anywhere] * 6,
+        in_specs=[anywhere] * 8,
         out_specs=(anywhere, anywhere),
         scratch_shapes=[
             vmem((members, rows, LANES), jnp.bfloat16),
             vmem((total_devices, rows, LANES), jnp.bfloat16),
             vmem((2, members, rows, LANES), jnp.bfloat16),
+            vmem((total_devices, 1, 3 * LANES), jnp.float32),
             vmem((2, total_devices, 1, 3 * LANES), jnp.float32),
+            pltpu.SMEM(frame_index.shape, jnp.int32),
+            vmem(velocity_index.shape, jnp.int32),
+            pltpu.SMEM(window.shape, jnp.int32),
+            vmem((total_devices, LANES), jnp.int32),
             vmem((LEVELS, 2 * rows, 2 * rows), jnp.bfloat16),
             vmem((2 * rows, rows), jnp.bfloat16),
             vmem((nx * side + 4, ny + 2, side, LANES), jnp.float32),
@@ -516,7 +545,7 @@
             vmem(translate_im.shape, jnp.bfloat16),
             vmem(eval_re.shape, jnp.bfloat16),
             vmem(eval_im.shape, jnp.bfloat16),
-            dma((4,)),
+            dma((7,)),
             dma((members,)),
             dma((members,)),
             dma((members,)),
@@ -531,7 +560,9 @@
         compiler_params=pltpu.CompilerParams(collective_id=0, has_side_effects=True),
     )(
         sources[0, 0].reshape(rows, columns),
-        extra,
+        frame_index,
+        velocity_index,
+        window,
         translate_re,
         translate_im,
         eval_re,
@@ -545,7 +576,8 @@
     nx, ny = mesh.shape["sx"], mesh.shape["sy"]
 
     def body(sources, *others):
-        if sources.shape[4] == nx * ny * LANES:
+        fits = others[3].shape[2] % LANES == 0
+        if fits and sources.shape[4] == nx * ny * LANES:
             return spread_on_device(nx, ny, sources, *others)
         return on_device(sources, *others)
 

time: 48.7 us -> 46.6 us (0.957)
  local copies, waits for them, and re-layouts: 1.4 us -> 0 us
  other arithmetic: 3.18 us -> 1.97 us
  Pallas kernels: 43.1 us -> 43.8 us
    unnamed x4 -> x0, local copies, waits for them, and re-layouts: 1.23 us -> none
    pallas_call x1, Pallas kernels: 43.1 us -> 43.8 us  [spread_on_device(): pl.pallas_call(functools.partial(spread_kernel, nx, ny), out_shape=(jax.S...]
    concatenate x1 -> x0, other arithmetic: 0.66 us -> none  [spread_on_device(): extra = jnp.concatenate([jnp.cos(angles), jnp.sin(angles), widths], axis=-1)]
where the time goes in v4:
time: 46.6 us; the launch traced here: 46.5 us
  Pallas kernels  43.8 us (94%)
  other arithmetic  1.97 us (4%)
  between operations  0.66 us (1%)
    pallas_call x1, Pallas kernels, spread_on_device(): pl.pallas_call(functools.partial(spread_kernel, nx, ny), out_shape=(jax.S...  43.8 us
    convert_element_type x1, other arithmetic, spread_on_device(): (out.astype(jnp.float32) + other.astype(jnp.float32)).astype(jnp.bfloat16)  1.97 us

profile of v4, /device:TPU:0, one launch (start us, length us, event | category | flops | bytes accessed | tf_op | source)
XLA Modules:
  0.0 46.5 jit_solution(8429810647179704759)
XLA Ops:
  0.7 43.8 %shard_map.82 = (bf16[8,8,4096]{2,1,0:T(8,128)(2,1)}, bf16[8,8,2048]{2,1,0:T(8,128)(2,1)}) custom-call(bf16[128,4096]{1,0:T(8,128)(2,1)} %bitcast.1, s32[1,1,16]{2,1,0:T(1,128)} %frame_hbm.1, s32[1,1,256]{2,1,0:T(1,128)} %velocity_hbm.1, s32[1,1]{1,0:T(1,128)S(6)} %copy.9.window_hbm, bf16[4,2,2,64,64]{4,3,2,1,0:T(8,128)(2,1)} %re_hbm.1, ...), custom_call_target="tpu_custom_call" | custom-call | tf_op jit(solution)/shard_map/pallas_call | solution.py:520
  44.5 2.0 %add_convert_fusion = bf16[8,8,4096]{2,1,0:T(8,128)(2,1)} fusion(bf16[8,8,4096]{2,1,0:T(8,128)(2,1)} %get-tuple-element.7, bf16[8,8,2048]{2,1,0:T(8,128)(2,1)} %get-tuple-element.8), kind=kLoop, calls=%fused_computation | loop fusion | flops 1048576 | bytes 1310720 | tf_op jit(solution)/shard_map/convert_element_type | solution.py:572
